TPU v7x, 32 devices: a whole 2x2x4 slice. The times are simulated.
32 devices in a mesh: tensor: 4 (over x, core), section: 2 (over y), dp: 4 (over z).
Axes of the slice: x: 2, y: 2, z: 4, core: 2. Of those that a mesh axis runs over, the one named last changes fastest.
Arguments:
- block_input: bfloat16 [4096, 6144], P(('section', 'dp')), may hold values from -6 to 6
- output_gradient: bfloat16 [4096, 6144], P(('section', 'dp')), may hold values from -6 to 6
- queries: bfloat16 [4096, 3072], P(('section', 'dp'), 'tensor'), may hold values from -8 to 8
- saved_keys: bfloat16 [4096, 3072], P(('section', 'dp'), 'tensor'), may hold values from -8 to 8
- values: bfloat16 [4096, 3072], P(('section', 'dp'), 'tensor'), may hold values from -6 to 6
- document_index: int32 [4096], P(('section', 'dp')), may hold values from 0 to 4095, as said below
- output_weight: bfloat16 [6144, 3072], P(('section', 'dp'), 'tensor'), may hold values from -0.109375 to 0.109375
- adapter_down_weight: bfloat16 [2, 6144, 128], P('section'), may hold values from -0.078125 to 0.078125
- adapter_up_weight: bfloat16 [2, 128, 3072], P('section', None, 'tensor'), may hold values from -0.5 to 0.5
Outputs:
- grad_out: float32 [6144, 3072], P(('section', 'dp'), 'tensor')
- grad_value_proj: float32 [6144, 3072], P(('section', 'dp'), 'tensor')
- grad_query: bfloat16 [4096, 3072], P(('section', 'dp'), 'tensor')
- grad_key: bfloat16 [4096, 3072], P(('section', 'dp'), 'tensor')
- grad_down: float32 [2, 6144, 128], P('section', 'dp')
- grad_up: float32 [2, 128, 3072], P('section', 'dp', 'tensor')
Inputs may be any that keep to these rules, and one draw needn't show every extreme that they name: `document_index`: ids never fall along the tokens; a document's id is the index of its first token, each block of 512 tokens starts a new document, and the last token is a document of its own.
All inputs are finite; a program needn't handle non-finite values.
Results may differ from a plain program's by a relative error of at most 0.015.
Values may be sent and summed in bfloat16 or wider, within the bound.
A program may use at most 192 MiB of HBM per device.

v0:
```python
import jax
import jax.numpy as jnp
from jax import lax
from jax.sharding import PartitionSpec as P

HD = 128


def attend(queries, saved_keys, values, attn_grad, document_index):
    token_rows = queries.shape[0]
    head_count = queries.shape[1] // HD
    score_scale = HD ** (-0.5)
    query_heads = queries.reshape(token_rows, head_count, HD)
    key_heads = saved_keys.reshape(token_rows, head_count, HD)
    value_heads = values.reshape(token_rows, head_count, HD)
    grad_heads = attn_grad.reshape(token_rows, head_count, HD)
    scores = (
        jnp.einsum("qhd,khd->hqk", query_heads, key_heads, preferred_element_type=jnp.float32)
        * score_scale
    )
    position = jnp.arange(token_rows, dtype=jnp.int32)
    allowed = (document_index[:, None] == document_index[None, :]) & (
        position[None, :] <= position[:, None]
    )
    scores = jnp.where(allowed[None], scores, jnp.float32(-1e30))
    top_score = jnp.max(scores, axis=-1, keepdims=True)
    expo = jnp.exp(scores - top_score)
    attn_probs = expo / jnp.sum(expo, axis=-1, keepdims=True)
    probs_half = attn_probs.astype(jnp.bfloat16)
    output = jnp.einsum(
        "hqk,khd->qhd", probs_half, value_heads, preferred_element_type=jnp.float32
    ).astype(jnp.bfloat16)
    value_gradient = jnp.einsum(
        "hqk,qhd->khd", probs_half, grad_heads, preferred_element_type=jnp.float32
    ).astype(jnp.bfloat16)
    grad_prob = jnp.einsum(
        "qhd,khd->hqk", grad_heads, value_heads, preferred_element_type=jnp.float32
    )
    row_delta = jnp.sum(attn_probs * grad_prob, axis=-1, keepdims=True)
    grad_score = (attn_probs * (grad_prob - row_delta) * score_scale).astype(jnp.bfloat16)
    grad_query = jnp.einsum(
        "hqk,khd->qhd", grad_score, key_heads, preferred_element_type=jnp.float32
    ).astype(jnp.bfloat16)
    grad_key = jnp.einsum(
        "hqk,qhd->khd", grad_score, query_heads, preferred_element_type=jnp.float32
    ).astype(jnp.bfloat16)
    width = head_count * HD
    return (
        output.reshape(token_rows, width),
        value_gradient.reshape(token_rows, width),
        grad_query.reshape(token_rows, width),
        grad_key.reshape(token_rows, width),
    )


def local(
    block_input,
    output_gradient,
    queries,
    saved_keys,
    values,
    document_index,
    output_weight,
    adapter_down_weight,
    adapter_up_weight,
):
    token_rows = block_input.shape[0]
    local_width = queries.shape[1]
    contract_rows = (((0,), (0,)), ((), ()))
    grad_cols = output_gradient
    attn_grad = jnp.dot(
        grad_cols,
        lax.all_gather(output_weight, ("section", "dp"), axis=0, tiled=True),
        preferred_element_type=jnp.float32,
    ).astype(jnp.bfloat16)
    output, value_gradient, grad_query, grad_key = attend(
        queries, saved_keys, values, attn_grad, document_index
    )
    grad_cols = output_gradient
    out_term = lax.dot_general(grad_cols, output, contract_rows, preferred_element_type=jnp.float32)
    value_term = lax.dot_general(
        block_input, value_gradient, contract_rows, preferred_element_type=jnp.float32
    )
    summed = lax.psum_scatter(
        jnp.concatenate([out_term, value_term], axis=1).astype(jnp.bfloat16),
        ("section", "dp"),
        scatter_dimension=0,
        tiled=True,
    ).astype(jnp.float32)
    narrow_product = jnp.dot(
        block_input, adapter_down_weight[0], preferred_element_type=jnp.float32
    ).astype(jnp.bfloat16)
    mix_part = lax.dot_general(
        value_gradient,
        adapter_up_weight[0],
        (((1,), (1,)), ((), ())),
        preferred_element_type=jnp.float32,
    )
    mix_term = lax.psum(mix_part.astype(jnp.bfloat16), "tensor")
    down_part = lax.dot_general(
        block_input, mix_term, contract_rows, preferred_element_type=jnp.float32
    )
    up_part = lax.dot_general(
        narrow_product, value_gradient, contract_rows, preferred_element_type=jnp.float32
    )
    down_total, up_total = (
        lax.psum_scatter(
            down_part.astype(jnp.bfloat16), "dp", scatter_dimension=0, tiled=True
        ).astype(jnp.float32),
        lax.psum_scatter(
            up_part.astype(jnp.bfloat16), "dp", scatter_dimension=0, tiled=True
        ).astype(jnp.float32),
    )
    token_factor = (token_rows * lax.axis_size("section") * lax.axis_size("dp")) ** (-0.5)
    adapter_factor = (token_rows * lax.axis_size("dp")) ** (-0.5)
    grad_out = summed[:, :local_width] * token_factor
    grad_value_proj = summed[:, local_width:] * token_factor
    return (
        grad_out,
        grad_value_proj,
        grad_query,
        grad_key,
        (down_total * adapter_factor)[None],
        (up_total * adapter_factor)[None],
    )


def solution(mesh):
    return jax.shard_map(
        local,
        mesh=mesh,
        in_specs=(
            P(("section", "dp"), None),
            P(("section", "dp"), None),
            P(("section", "dp"), "tensor"),
            P(("section", "dp"), "tensor"),
            P(("section", "dp"), "tensor"),
            P(("section", "dp")),
            P(("section", "dp"), "tensor"),
            P("section", None, None),
            P("section", None, "tensor"),
        ),
        out_specs=(
            P(("section", "dp"), "tensor"),
            P(("section", "dp"), "tensor"),
            P(("section", "dp"), "tensor"),
            P(("section", "dp"), "tensor"),
            P("section", "dp", None),
            P("section", "dp", "tensor"),
        ),
        check_vma=False,
    )
```

profile of v0, /device:TPU:0, one launch (start us, length us, event | category | flops | bytes accessed | tf_op | source)
XLA Modules:
  0.0 589.8 jit_solution(15455212225179713954)
XLA Ops:
  7.2 0.0 copy-start
  7.2 0.0 all-gather.2.cloned.1.call-start
  7.2 0.7 all-gather.2.cloned.1.call-update
  7.9 0.0 all-reduce.2.cloned.1.call-start
  8.0 2.3 copy.32
  10.3 1.4 copy.33
  11.7 0.0 copy-start.2
  11.7 1.7 copy.36
  13.4 1.0 fusion.41
  14.3 6.2 %fusion.51 = (f32[6,512]{1,0:T(8,128)S(1)}, f32[6,512,512]{1,2,0:T(8,128)}) fusion(pred[512,512]{0,1:T(8,128)(4,1)S(1)} %fusion.41, bf16[512,6,128]{0,2,1:T(8,128)(2,1)} %bitcast.63, bf16[512,6,128]{0,2,1:T(8,128)(2,1)S(1)} %bitcast.61), kind=kOutput, calls=%fused_computation.49 | convolution fusion | flops 408945152 | bytes 8138752 | tf_op jit(solution)/shard_map/sub | solution.py:27
  20.5 4.9 fusion.24
  25.5 125.5 %all-gather.2.cloned.1.call-done = bf16[6144,768]{1,0:T(8,128)(2,1)} async-done(((bf16[768,768]{1,0:T(8,128)(2,1)}), bf16[6144,768]{1,0:T(8,128)(2,1)}) %all-gather.2.cloned.1.call-update) | async-done | bytes 9437200 | tf_op jit(solution)/shard_map/all_gather | solution.py:73
  150.9 10.6 %convolution_convert_fusion.3 = bf16[512,768]{1,0:T(8,128)(2,1)} fusion(bf16[512,6144]{1,0:T(8,128)(2,1)} %param.10, bf16[6144,768]{1,0:T(8,128)(2,1)} %all-gather.2.cloned.1.call-done), kind=kOutput, calls=%fused_computation.33 | convolution fusion | flops 4832231424 | bytes 16515072 | tf_op jit(solution)/shard_map/dot_general | solution.py:71
  161.5 1.4 copy.38
  162.9 0.0 copy-start.7
  162.9 4.0 fusion.27
  166.9 0.0 copy-start.5
  166.9 0.9 copy-done.5
  167.8 1.1 convolution_convert_fusion.5
  168.9 0.0 all-reduce.2.cloned.1.call-update
  168.9 0.0 reduce-scatter.8.cloned.1.call-start
  169.0 6.1 %convolution_convert_fusion.4 = bf16[128,768]{1,0:T(8,128)(2,1)} fusion(bf16[512,768]{0,1:T(8,128)(2,1)} %bitcast.68, bf16[512,6144]{1,0:T(8,128)(2,1)} %param.9, bf16[1,6144,128]{2,1,0:T(8,128)(2,1)S(1)} %copy-done), kind=kOutput, calls=%fused_computation.34 | convolution fusion | flops 906133504 | bytes 8847360 | tf_op jit(solution)/shard_map/dot_general | solution.py:103
  175.1 0.0 reduce-scatter.8.cloned.1.call-update
  175.1 0.0 copy-start.8
  175.1 0.0 reduce-scatter.6.cloned.1.call-start
  175.1 23.5 %all-reduce.2.cloned.1.call-done = bf16[512,128]{1,0:T(8,128)(2,1)} async-done(((bf16[512,128]{1,0:T(8,128)(2,1)}), bf16[512,128]{1,0:T(8,128)(2,1)}) %all-reduce.2.cloned.1.call-update) | async-done | bytes 131088 | tf_op jit(solution)/shard_map/psum | solution.py:99
  198.6 5.0 fusion.4
  203.7 0.0 reduce-scatter.6.cloned.1.call-update
  203.7 0.2 reduce-scatter.4.cloned.1.call-start
  203.9 0.0 copy-start.6
  203.9 8.1 %fusion.2 = bf16[6144,768]{0,1:T(8,128)(2,1)S(1)} fusion(bf16[512,768]{0,1:T(8,128)(2,1)S(1)} %bitcast.70, bf16[512,6144]{1,0:T(8,128)(2,1)} %param.10), kind=kOutput, calls=%fused_computation.5 | convolution fusion | flops 4836556800 | bytes 16515072 | tf_op jit(solution)/shard_map/dot_general | solution.py:80
  212.1 8.1 %fusion.3 = bf16[6144,768]{0,1:T(8,128)(2,1)S(1)} fusion(bf16[512,768]{0,1:T(8,128)(2,1)S(1)} %bitcast.69, bf16[512,6144]{1,0:T(8,128)(2,1)} %param.9), kind=kOutput, calls=%fused_computation.6 | convolution fusion | flops 4836556800 | bytes 16515072 | tf_op jit(solution)/shard_map/dot_general | solution.py:81
  220.2 21.3 %pad_maximum_fusion = bf16[6144,1536]{0,1:T(8,128)(2,1)} fusion(bf16[6144,768]{0,1:T(8,128)(2,1)S(1)} %fusion.3, bf16[6144,768]{0,1:T(8,128)(2,1)S(1)} %fusion.2), kind=kLoop, calls=%fused_computation.2 | loop fusion | flops 37748736 | bytes 37748736 | tf_op jit(solution)/shard_map/concatenate | solution.py:85
  241.4 0.0 reduce-scatter.4.cloned.1.call-update
  241.5 0.0 copy-start.4
  241.5 3.7 fusion.52
  245.2 9.9 %fusion.33 = bf16[6,512,128]{1,2,0:T(8,128)(2,1)S(1)} fusion(bf16[512,6,128]{0,2,1:T(8,128)(2,1)S(1)} %bitcast.64, f32[6,512,512]{1,2,0:T(8,128)} %fusion.52, f32[6,512,512]{1,2,0:T(8,128)} %get-tuple-element.21, f32[6,512]{1,0:T(8,128)S(1)} %get-tuple-element.20), kind=kOutput, calls=%fused_computation.32 | convolution fusion | flops 414060032 | bytes 14168064 | tf_op jit(solution)/shard_map/hqk,qhd->khd/dot_general | solution.py:44
  255.1 1.2 copy.47
  256.3 10.9 %fusion.30 = bf16[6,512,128]{1,2,0:T(8,128)(2,1)S(1)} fusion(bf16[512,6,128]{0,2,1:T(8,128)(2,1)S(1)} %bitcast.62, f32[6,512,512]{1,2,0:T(8,128)} %fusion.52, f32[6,512,512]{1,2,0:T(8,128)} %get-tuple-element.21, f32[6,512]{1,0:T(8,128)S(1)} %get-tuple-element.20), kind=kOutput, calls=%fused_computation.31 | convolution fusion | flops 414060032 | bytes 14168064 | tf_op jit(solution)/shard_map/hqk,khd->qhd/dot_general | solution.py:41
  267.2 1.2 copy.46
  268.4 1.4 multiply_bitcast_fusion.1
  269.8 1.1 multiply_bitcast_fusion
  270.9 1.1 copy.48
  272.1 300.6 %reduce-scatter.4.cloned.1.call-done = bf16[768,1536]{0,1:T(8,128)(2,1)} async-done(((bf16[6144,1536]{0,1:T(8,128)(2,1)}), bf16[768,1536]{0,1:T(8,128)(2,1)}) %reduce-scatter.4.cloned.1.call-update) | async-done | bytes 2359312 | tf_op jit(solution)/shard_map/reduce_scatter | solution.py:84
  572.7 2.0 convert_element_type.64
  574.7 2.5 slice_multiply_fusion
  577.2 3.0 copy.45
  580.3 3.0 copy.44
  (12 shorter events, 0.0 us)
Async XLA Ops:
  7.2 161.8 %copy-start = (bf16[1,6144,128]{2,1,0:T(8,128)(2,1)S(1)}, bf16[1,6144,128]{2,1,0:T(8,128)(2,1)}, u32[]{:S(2)}) copy-start(bf16[1,6144,128]{2,1,0:T(8,128)(2,1)} %param.16) | copy-start | bytes 4718596
  7.2 143.7 %all-gather.2.cloned.1.call-start = ((), (), s32[]{:S(2)}) async-start(), calls=%async_computation.3 | async-start | bytes 10616832 | tf_op jit(solution)/shard_map/all_gather | solution.py:73
  7.9 190.7 %all-reduce.2.cloned.1.call-start = ((), (), s32[]{:S(2)}) async-start(), calls=%async_computation.5 | async-start | bytes 262144 | tf_op jit(solution)/shard_map/psum | solution.py:99
  11.7 8.8 %copy-start.2 = (bf16[512,768]{0,1:T(8,128)(2,1)}, bf16[512,768]{0,1:T(8,128)(2,1)S(1)}, u32[]{:S(2)}) copy-start(bf16[512,768]{0,1:T(8,128)(2,1)S(1)} %copy.33) | copy-start | bytes 2359300
  162.9 4.9 copy-start.7
  166.9 0.9 copy-start.5
  168.9 99.5 %reduce-scatter.8.cloned.1.call-start = ((), (), s32[]{:S(2)}) async-start(), calls=%async_computation.7 | async-start | bytes 245760 | tf_op jit(solution)/shard_map/reduce_scatter | solution.py:110
  175.1 28.8 %copy-start.8 = (bf16[6,512,128]{1,2,0:T(8,128)(2,1)S(1)}, bf16[6,512,128]{1,2,0:T(8,128)(2,1)}, u32[]{:S(2)}) copy-start(bf16[6,512,128]{1,2,0:T(8,128)(2,1)} %fusion.24) | copy-start | bytes 2359300
  175.1 94.8 %reduce-scatter.6.cloned.1.call-start = ((), (), s32[]{:S(2)}) async-start(), calls=%async_computation.6 | async-start | bytes 1966080 | tf_op jit(solution)/shard_map/reduce_scatter | solution.py:107
  203.7 369.0 %reduce-scatter.4.cloned.1.call-start = ((), (), s32[]{:S(2)}) async-start(), calls=%async_computation.4 | async-start | bytes 21233664 | tf_op jit(solution)/shard_map/reduce_scatter | solution.py:84
  203.9 8.1 %copy-start.6 = (bf16[6,128,512]{2,1,0:T(8,128)(2,1)S(1)}, bf16[6,128,512]{2,1,0:T(8,128)(2,1)}, u32[]{:S(2)}) copy-start(bf16[6,128,512]{2,1,0:T(8,128)(2,1)} %copy-done.5) | copy-start | bytes 2359300
  241.5 3.7 copy-start.4
  245.2 11.1 %copy-start.3 = (bf16[512,768]{0,1:T(8,128)(2,1)S(1)}, bf16[512,768]{0,1:T(8,128)(2,1)}, u32[]{:S(2)}) copy-start(bf16[512,768]{0,1:T(8,128)(2,1)} %copy-done.2) | copy-start | bytes 2359300
  574.7 8.6 %copy-start.1 = (bf16[1,6144,128]{2,1,0:T(8,128)(2,1)S(1)}, bf16[1,6144,128]{2,1,0:T(8,128)(2,1)}, u32[]{:S(2)}) copy-start(bf16[1,6144,128]{2,1,0:T(8,128)(2,1)} %param.16) | copy-start | bytes 4718596
Sparse Core Ops, SparseCore 0:
  10.1 140.7 all-gather.1
  169.0 29.5 all-reduce.1
  201.0 19.3 reduce-scatter.7
  223.1 33.4 reduce-scatter.5
  260.3 312.2 reduce-scatter.3
where the time goes:
time: 590 us
  waiting for transfers between devices  450 us (76%)
  matrix products  78.6 us (13%)
  other arithmetic  29.3 us (5%)
  local copies, waits for them, and re-layouts  17.3 us (3%)
  between operations  13.9 us (2%)
    reduce_scatter x1, waiting for transfers between devices, local(): lax.psum_scatter(jnp.concatenate([out_term, value_term], axis=1).astype(j...  301 us
    all_gather x1, waiting for transfers between devices, local(): lax.all_gather(output_weight, ('section', 'dp'), axis=0, tiled=True)  125 us
    psum x1, waiting for transfers between devices, local(): mix_term = lax.psum(mix_part.astype(jnp.bfloat16), 'tensor')  23.5 us
    concatenate x1, other arithmetic, local(): jnp.concatenate([out_term, value_term], axis=1).astype(jnp.bfloat16)  21.3 us
    unnamed x26, local copies, waits for them, and re-layouts  15.9 us
  transfers between devices with their start and end apart: 5, of which 3 were waited for; matrix products, arithmetic and copies ran while one was open for 16% of the time, Pallas kernels for 0%

commit v1 on v0

--- a/solution.py
+++ b/solution.py
@@ -96,7 +96,9 @@
         (((1,), (1,)), ((), ())),
         preferred_element_type=jnp.float32,
     )
-    mix_term = lax.psum(mix_part.astype(jnp.bfloat16), "tensor")
+    inp = mix_part.astype(jnp.bfloat16)
+    x_now = lax.all_gather(inp, "tensor")
+    mix_term = jnp.sum(x_now, axis=0)
     down_part = lax.dot_general(
         block_input, mix_term, contract_rows, preferred_element_type=jnp.float32
     )

time: 590 us -> 563 us (0.954)
  waiting for transfers between devices: 450 us -> 416 us
  blocking collectives: 0 us -> 7.17 us
    psum x1 -> x0, waiting for transfers between devices: 23.5 us -> none  [local(): mix_term = lax.psum(mix_part.astype(jnp.bfloat16), 'tensor')]
    reduce_scatter x1, waiting for transfers between devices: 301 us -> 290 us  [local(): lax.psum_scatter(jnp.concatenate([out_term, value_term], axis=1).astype(j...]
    all_gather x0 -> x1, blocking collectives: none -> 7.17 us  [local(): x_now = lax.all_gather(inp, 'tensor')]
  transfers between devices with their start and end apart: 5 -> 4, of which waited for: 3 -> 2; matrix products, arithmetic and copies ran while one was open for 16% -> 16% of each run, Pallas kernels for 0% -> 0%
where the time goes in v1:
time: 563 us; the launch traced here: 562 us
  waiting for transfers between devices  416 us (74%)
  matrix products  77.9 us (14%)
  other arithmetic  29.3 us (5%)
  local copies, waits for them, and re-layouts  17.3 us (3%)
  between operations  13.9 us (2%)
  blocking collectives  7.17 us (1%)
    reduce_scatter x1, waiting for transfers between devices, local(): lax.psum_scatter(jnp.concatenate([out_term, value_term], axis=1).astype(j...  290 us
    all_gather x1, waiting for transfers between devices, local(): lax.all_gather(output_weight, ('section', 'dp'), axis=0, tiled=True)  125 us
    concatenate x1, other arithmetic, local(): jnp.concatenate([out_term, value_term], axis=1).astype(jnp.bfloat16)  21.2 us
    unnamed x26, local copies, waits for them, and re-layouts  15.9 us
  transfers between devices with their start and end apart: 4, of which 2 were waited for; matrix products, arithmetic and copies ran while one was open for 16% of the time, Pallas kernels for 0%

profile of v1, /device:TPU:0, one launch (start us, length us, event | category | flops | bytes accessed | tf_op | source)
XLA Modules:
  0.0 562.2 jit_solution(18219163821233922454)
XLA Ops:
  7.2 0.0 copy-start
  7.2 0.0 all-gather.3.cloned.1.call-start
  7.2 0.7 all-gather.3.cloned.1.call-update
  7.9 0.0 reduce-scatter.8.cloned.1.call-start
  8.0 2.3 copy.32
  10.3 1.4 copy.33
  11.7 0.0 copy-start.2
  11.7 1.7 copy.36
  13.4 1.0 fusion.41
  14.3 6.2 %fusion.51 = (f32[6,512]{1,0:T(8,128)S(1)}, f32[6,512,512]{1,2,0:T(8,128)}) fusion(pred[512,512]{0,1:T(8,128)(4,1)S(1)} %fusion.41, bf16[512,6,128]{0,2,1:T(8,128)(2,1)} %bitcast.65, bf16[512,6,128]{0,2,1:T(8,128)(2,1)S(1)} %bitcast.63), kind=kOutput, calls=%fused_computation.49 | convolution fusion | flops 408945152 | bytes 8138752 | tf_op jit(solution)/shard_map/sub | solution.py:27
  20.5 4.9 fusion.24
  25.5 125.5 %all-gather.3.cloned.1.call-done = bf16[6144,768]{1,0:T(8,128)(2,1)} async-done(((bf16[768,768]{1,0:T(8,128)(2,1)}), bf16[6144,768]{1,0:T(8,128)(2,1)}) %all-gather.3.cloned.1.call-update) | async-done | bytes 9437200 | tf_op jit(solution)/shard_map/all_gather | solution.py:73
  150.9 10.6 %convolution_convert_fusion.3 = bf16[512,768]{1,0:T(8,128)(2,1)} fusion(bf16[512,6144]{1,0:T(8,128)(2,1)} %param.10, bf16[6144,768]{1,0:T(8,128)(2,1)} %all-gather.3.cloned.1.call-done), kind=kOutput, calls=%fused_computation.33 | convolution fusion | flops 4832231424 | bytes 16515072 | tf_op jit(solution)/shard_map/dot_general | solution.py:71
  161.5 1.4 copy.38
  162.9 0.0 copy-start.7
  162.9 4.0 fusion.27
  166.9 0.0 copy-start.5
  166.9 0.9 copy-done.5
  167.8 0.4 convolution_convert_fusion.5
  168.2 6.1 %convolution_convert_fusion.4 = bf16[128,768]{1,0:T(8,128)(2,1)} fusion(bf16[512,768]{0,1:T(8,128)(2,1)} %bitcast.70, bf16[512,6144]{1,0:T(8,128)(2,1)} %param.9, bf16[1,6144,128]{2,1,0:T(8,128)(2,1)S(1)} %copy-done), kind=kOutput, calls=%fused_computation.34 | convolution fusion | flops 906133504 | bytes 8847360 | tf_op jit(solution)/shard_map/dot_general | solution.py:105
  174.3 0.0 reduce-scatter.8.cloned.1.call-update
  174.3 0.0 reduce-scatter.6.cloned.1.call-start
  174.4 7.2 %all-gather = bf16[2048,128]{1,0:T(8,128)(2,1)S(1)} all-gather(bf16[512,128]{1,0:T(8,128)(2,1)S(1)} %convolution_convert_fusion.5), channel_id=2, replica_groups=mesh['tensor'=4,'section'=2,'dp'=4] {'tensor'}, dimensions={0}, use_global_device_ids=true | all-gather | bytes 655360 | tf_op jit(solution)/shard_map/all_gather | solution.py:100
  181.6 0.1 reduce_sum.32
  181.6 0.0 copy-start.8
  181.6 5.0 fusion.4
  186.7 0.0 reduce-scatter.6.cloned.1.call-update
  186.7 0.2 reduce-scatter.4.cloned.1.call-start
  186.9 0.0 copy-start.6
  187.0 8.1 %fusion.2 = bf16[6144,768]{0,1:T(8,128)(2,1)S(1)} fusion(bf16[512,768]{0,1:T(8,128)(2,1)S(1)} %bitcast.72, bf16[512,6144]{1,0:T(8,128)(2,1)} %param.10), kind=kOutput, calls=%fused_computation.5 | convolution fusion | flops 4836556800 | bytes 16515072 | tf_op jit(solution)/shard_map/dot_general | solution.py:80
  195.1 8.1 %fusion.3 = bf16[6144,768]{0,1:T(8,128)(2,1)S(1)} fusion(bf16[512,768]{0,1:T(8,128)(2,1)S(1)} %bitcast.71, bf16[512,6144]{1,0:T(8,128)(2,1)} %param.9), kind=kOutput, calls=%fused_computation.6 | convolution fusion | flops 4836556800 | bytes 16515072 | tf_op jit(solution)/shard_map/dot_general | solution.py:81
  203.1 21.2 %pad_maximum_fusion = bf16[6144,1536]{0,1:T(8,128)(2,1)} fusion(bf16[6144,768]{0,1:T(8,128)(2,1)S(1)} %fusion.3, bf16[6144,768]{0,1:T(8,128)(2,1)S(1)} %fusion.2), kind=kLoop, calls=%fused_computation.2 | loop fusion | flops 37748736 | bytes 37748736 | tf_op jit(solution)/shard_map/concatenate | solution.py:85
  224.4 0.0 reduce-scatter.4.cloned.1.call-update
  224.4 0.0 copy-start.4
  224.4 3.7 fusion.52
  228.2 9.8 %fusion.33 = bf16[6,512,128]{1,2,0:T(8,128)(2,1)S(1)} fusion(bf16[512,6,128]{0,2,1:T(8,128)(2,1)S(1)} %bitcast.66, f32[6,512,512]{1,2,0:T(8,128)} %fusion.52, f32[6,512,512]{1,2,0:T(8,128)} %get-tuple-element.21, f32[6,512]{1,0:T(8,128)S(1)} %get-tuple-element.20), kind=kOutput, calls=%fused_computation.32 | convolution fusion | flops 414060032 | bytes 14168064 | tf_op jit(solution)/shard_map/hqk,qhd->khd/dot_general | solution.py:44
  238.0 1.2 copy.47
  239.1 11.0 %fusion.30 = bf16[6,512,128]{1,2,0:T(8,128)(2,1)S(1)} fusion(bf16[512,6,128]{0,2,1:T(8,128)(2,1)S(1)} %bitcast.64, f32[6,512,512]{1,2,0:T(8,128)} %fusion.52, f32[6,512,512]{1,2,0:T(8,128)} %get-tuple-element.21, f32[6,512]{1,0:T(8,128)S(1)} %get-tuple-element.20), kind=kOutput, calls=%fused_computation.31 | convolution fusion | flops 414060032 | bytes 14168064 | tf_op jit(solution)/shard_map/hqk,khd->qhd/dot_general | solution.py:41
  250.2 1.2 copy.46
  251.3 1.4 multiply_bitcast_fusion.1
  252.8 1.1 multiply_bitcast_fusion
  253.9 1.1 copy.48
  255.0 290.0 %reduce-scatter.4.cloned.1.call-done = bf16[768,1536]{0,1:T(8,128)(2,1)} async-done(((bf16[6144,1536]{0,1:T(8,128)(2,1)}), bf16[768,1536]{0,1:T(8,128)(2,1)}) %reduce-scatter.4.cloned.1.call-update) | async-done | bytes 2359312 | tf_op jit(solution)/shard_map/reduce_scatter | solution.py:84
  545.1 2.0 convert_element_type.66
  547.1 0.0 copy-start.1
  547.1 2.5 slice_multiply_fusion
  549.6 3.0 copy.45
  552.6 3.0 copy.44
  (11 shorter events, 0.0 us)
Async XLA Ops:
  7.2 161.1 %copy-start = (bf16[1,6144,128]{2,1,0:T(8,128)(2,1)S(1)}, bf16[1,6144,128]{2,1,0:T(8,128)(2,1)}, u32[]{:S(2)}) copy-start(bf16[1,6144,128]{2,1,0:T(8,128)(2,1)} %param.16) | copy-start | bytes 4718596
  7.2 143.7 %all-gather.3.cloned.1.call-start = ((), (), s32[]{:S(2)}) async-start(), calls=%async_computation.3 | async-start | bytes 10616832 | tf_op jit(solution)/shard_map/all_gather | solution.py:73
  7.9 243.4 %reduce-scatter.8.cloned.1.call-start = ((), (), s32[]{:S(2)}) async-start(), calls=%async_computation.6 | async-start | bytes 245760 | tf_op jit(solution)/shard_map/reduce_scatter | solution.py:112
  11.7 8.8 %copy-start.2 = (bf16[512,768]{0,1:T(8,128)(2,1)}, bf16[512,768]{0,1:T(8,128)(2,1)S(1)}, u32[]{:S(2)}) copy-start(bf16[512,768]{0,1:T(8,128)(2,1)S(1)} %copy.33) | copy-start | bytes 2359300
  162.9 4.9 copy-start.7
  166.9 0.9 copy-start.5
  174.3 78.4 %reduce-scatter.6.cloned.1.call-start = ((), (), s32[]{:S(2)}) async-start(), calls=%async_computation.5 | async-start | bytes 1966080 | tf_op jit(solution)/shard_map/reduce_scatter | solution.py:109
  181.6 5.3 copy-start.8
  186.7 358.4 %reduce-scatter.4.cloned.1.call-start = ((), (), s32[]{:S(2)}) async-start(), calls=%async_computation.4 | async-start | bytes 21233664 | tf_op jit(solution)/shard_map/reduce_scatter | solution.py:84
  186.9 8.1 %copy-start.6 = (bf16[6,128,512]{2,1,0:T(8,128)(2,1)S(1)}, bf16[6,128,512]{2,1,0:T(8,128)(2,1)}, u32[]{:S(2)}) copy-start(bf16[6,128,512]{2,1,0:T(8,128)(2,1)} %copy-done.5) | copy-start | bytes 2359300
  224.4 3.8 copy-start.4
  228.2 11.0 %copy-start.3 = (bf16[512,768]{0,1:T(8,128)(2,1)S(1)}, bf16[512,768]{0,1:T(8,128)(2,1)}, u32[]{:S(2)}) copy-start(bf16[512,768]{0,1:T(8,128)(2,1)} %copy-done.2) | copy-start | bytes 2359300
  547.1 8.6 %copy-start.1 = (bf16[1,6144,128]{2,1,0:T(8,128)(2,1)S(1)}, bf16[1,6144,128]{2,1,0:T(8,128)(2,1)}, u32[]{:S(2)}) copy-start(bf16[1,6144,128]{2,1,0:T(8,128)(2,1)} %param.16) | copy-start | bytes 4718596
Sparse Core Ops, SparseCore 0:
  10.1 140.7 all-gather.2
  174.5 17.5 reduce-scatter.7
  195.1 33.4 reduce-scatter.5
  232.8 312.2 reduce-scatter.3
